TPU v7x, 256 devices: a whole 4x4x8 slice. The times are simulated.
256 devices in a mesh: ens: 8 (over y, z_hi), tile: 32 (over z_lo, x, core).
Axes of the slice: x: 4, y: 4, z: 8 (z_hi: 2, z_lo: 4; z = z_hi * 4 + z_lo), core: 2. Of those that a mesh axis runs over, the one named last changes fastest.
Arguments:
- fields: bfloat16 [8, 32, 200, 8, 128], P('ens', 'tile'), may hold values from -6 to 6
- target: bfloat16 [8, 32, 200, 8, 128], P('ens', 'tile'), may hold values from -6 to 6
- wet_levels: int32 [32, 8, 128], P('tile'), may hold values from 0 to 19, as said below
- tile_links: int32 [32, 5], replicated, may hold values from -1 to 31, as said below
- tile_owner: int32 [32], replicated, may hold values from 0 to 31, as said below
- kernel: float32 [200, 49], replicated, may hold values from -0.875 to 0.875
- norm_gain: float32 [200], replicated, may hold values from 0.5 to 1.5
- weight_in: bfloat16 [200, 800], replicated, may hold values from -0.4375 to 0.4375
- weight_out: bfloat16 [800, 200], replicated, may hold values from -0.21875 to 0.21875
- layer_scale: float32 [200], replicated, may hold values from 0.25 to 1
Outputs:
- block_out: bfloat16 [8, 32, 200, 8, 128], P('ens', 'tile')
- grad_in: float32 [200, 800], replicated
- grad_out: float32 [800, 200], replicated
- grad_kernel: float32 [200, 49], replicated
Inputs may be any that keep to these rules, and one draw needn't show every extreme that they name: `wet_levels`: 0 is land; a cell is wet at the levels below its value. `tile_links`: the kept tiles are the kept blocks of a grid 8 tiles wide, numbered row by row from the south. West and east wrap around within a grid row; the southmost row has no south neighbour; the northmost row is complete, its north neighbour is the tile of the same row in the mirrored column 7 - column, and only it has flag 1 in column 4; -1 marks a missing neighbour. Column 4 is 0 or 1. `tile_owner`: a permutation.
All inputs are finite; a program needn't handle non-finite values.
Results may differ from a plain program's by a relative error of at most 0.005.
Values may be sent and summed in bfloat16 or wider, within the bound.
No kernel may reach another device: no remote copies, remote signals or barrier semaphores. Data moves between devices by JAX's collectives and lax.ppermute only.
A program may use at most 192 MiB of HBM per device.

v0:
```python
import jax
import jax.numpy as jnp
from jax import lax
from jax.sharding import PartitionSpec as P

LEVELS = 19
root_half = 0.7071067811865476
gauss_norm = 0.3989422804014327
norm_epsilon = 1e-06


def gelu_value(values):
    return 0.5 * values * (1.0 + lax.erf(values * root_half))


def gelu_slope(values):
    return (
        0.5 * (1.0 + lax.erf(values * root_half))
        + values * jnp.exp(-0.5 * values * values) * gauss_norm
    )


def take_slot(held, pieces, slot_id):
    piece_count = pieces.shape[0]
    inside = (slot_id >= 0) & (slot_id >= 0) & (slot_id < piece_count)
    taken = lax.dynamic_index_in_dim(
        pieces, jnp.clip(slot_id, 0, piece_count - 1), 0, keepdims=False
    )
    return jnp.where(inside, taken, held)


def local(
    fields,
    target,
    wet_levels,
    tile_links,
    tile_owner,
    kernel,
    norm_gain,
    weight_in,
    weight_out,
    layer_scale,
):
    members, _, channels, row_count, col_count = fields.shape
    tile_count = tile_owner.shape[0]
    own_slot = lax.axis_index("tile")
    own_tile = jnp.sum(
        jnp.where(tile_owner == own_slot, jnp.arange(tile_count, dtype=jnp.int32), 0)
    )
    level_of = jnp.arange(channels, dtype=jnp.int32) * LEVELS // channels
    wet_mask = wet_levels[0][None, :, :] > level_of[:, None, None]
    own_input = fields[:, 0]
    masked = jnp.where(wet_mask[None], own_input, jnp.zeros_like(own_input))
    entry_total = jnp.float32(
        members * lax.axis_size("ens") * tile_count * channels * row_count * col_count
    )

    def link_of(tile_id, column):
        return jnp.where(tile_id >= 0, tile_links[jnp.clip(tile_id, 0, tile_count - 1), column], -1)

    def slot_of(tile_id):
        return jnp.where(tile_id >= 0, tile_owner[jnp.clip(tile_id, 0, tile_count - 1)], -1)

    north_slot = slot_of(link_of(own_tile, 0))
    south_slot = slot_of(link_of(own_tile, 1))
    own_fold = link_of(own_tile, 4)
    west_tile = link_of(own_tile, 2)
    east_tile = link_of(own_tile, 3)
    west_slot = slot_of(west_tile)
    east_slot = slot_of(east_tile)
    zero_rows = jnp.zeros((members, channels, 3, col_count), jnp.bfloat16)
    row_strips = jnp.stack([masked[:, :, :3, :], masked[:, :, row_count - 3 :, :]], axis=0)[None]
    held = (zero_rows, zero_rows, zero_rows)
    pieces = lax.all_gather(row_strips, "tile", axis=0, tiled=True)
    lower_rows = take_slot(held[0], pieces[:, 0], north_slot)
    upper_rows = take_slot(held[1], pieces[:, 1], north_slot)
    below_rows = take_slot(held[2], pieces[:, 1], south_slot)
    north_rows = jnp.where(own_fold == 1, jnp.flip(upper_rows, (2, 3)), lower_rows)
    center = jnp.concatenate([below_rows, masked, north_rows], axis=2)
    side_cols = jnp.swapaxes(
        jnp.stack([center[..., :3], center[..., col_count - 3 :]], axis=0), 3, 4
    )[None]
    zero_cols = jnp.zeros((members, channels, 3, row_count + 6), jnp.bfloat16)
    held = (zero_cols, zero_cols)
    pieces = lax.all_gather(side_cols, "tile", axis=0, tiled=True)
    west_part = take_slot(held[0], pieces[:, 1], west_slot)
    east_part = take_slot(held[1], pieces[:, 0], east_slot)
    west_cols = jnp.swapaxes(west_part, 2, 3)
    east_cols = jnp.swapaxes(east_part, 2, 3)
    extended = jnp.concatenate([west_cols, center, east_cols], axis=3).astype(jnp.float32)
    conv_out = jnp.zeros((members, channels, row_count, col_count), jnp.float32)
    for row_off in range(7):
        for col_off in range(7):
            conv_out = (
                conv_out
                + kernel[:, 7 * row_off + col_off][None, :, None, None]
                * extended[:, :, row_off : row_off + row_count, col_off : col_off + col_count]
            )
    chan_mean = jnp.mean(conv_out, axis=1, keepdims=True)
    chan_var = jnp.mean((conv_out - chan_mean) ** 2, axis=1, keepdims=True)
    inv_std = 1.0 / jnp.sqrt(chan_var + norm_epsilon)
    centred = (conv_out - chan_mean) * inv_std
    gain_wide = norm_gain[None, :, None, None]
    scale_wide = layer_scale[None, :, None, None]
    normed = (centred * gain_wide).astype(jnp.bfloat16)
    flat_norm = normed.reshape(members, channels, row_count * col_count)
    hidden = jnp.einsum("ch,ecp->ehp", weight_in, flat_norm, preferred_element_type=jnp.float32)
    activated = gelu_value(hidden).astype(jnp.bfloat16)
    mlp_out = jnp.einsum("hc,ehp->ecp", weight_out, activated, preferred_element_type=jnp.float32)
    mlp_out = mlp_out.reshape(members, channels, row_count, col_count)
    block_out = (masked.astype(jnp.float32) + scale_wide * mlp_out).astype(jnp.bfloat16)
    misfit = jnp.where(
        wet_mask[None], block_out.astype(jnp.float32) - target[:, 0].astype(jnp.float32), 0.0
    )
    grad_mlp = (
        (2.0 * scale_wide * misfit)
        .astype(jnp.bfloat16)
        .reshape(members, channels, row_count * col_count)
    )
    part_out = jnp.einsum("ehp,ecp->hc", activated, grad_mlp, preferred_element_type=jnp.float32)
    grad_act = jnp.einsum("hc,ecp->ehp", weight_out, grad_mlp, preferred_element_type=jnp.float32)
    grad_hidden = (grad_act * gelu_slope(hidden)).astype(jnp.bfloat16)
    part_in = jnp.einsum("ecp,ehp->ch", flat_norm, grad_hidden, preferred_element_type=jnp.float32)
    grad_normed = jnp.einsum(
        "ch,ehp->ecp", weight_in, grad_hidden, preferred_element_type=jnp.float32
    )
    grad_scaled = grad_normed.reshape(members, channels, row_count, col_count) * gain_wide
    grad_conv = (
        grad_scaled
        - jnp.mean(grad_scaled, axis=1, keepdims=True)
        - centred * jnp.mean(grad_scaled * centred, axis=1, keepdims=True)
    ) * inv_std
    kernel_terms = []
    for row_off in range(7):
        for col_off in range(7):
            kernel_terms.append(
                jnp.sum(
                    grad_conv
                    * extended[:, :, row_off : row_off + row_count, col_off : col_off + col_count],
                    axis=(0, 2, 3),
                )
            )
    part_kernel = jnp.stack(kernel_terms, axis=1)
    sum_in, sum_out, sum_kernel = lax.psum((part_in, part_out, part_kernel), ("ens", "tile"))
    return (
        block_out[:, None],
        sum_in / entry_total,
        sum_out / entry_total,
        sum_kernel / entry_total,
    )


def solution(mesh):
    placed = (
        P("ens", "tile", None, None, None),
        P("ens", "tile", None, None, None),
        P("tile", None, None),
        P(),
        P(),
        P(),
        P(),
        P(),
        P(),
        P(),
    )
    return jax.shard_map(
        local,
        mesh=mesh,
        in_specs=placed,
        out_specs=(P("ens", "tile", None, None, None), P(), P(), P()),
        check_vma=False,
    )
```

profile of v0, /device:TPU:8, one launch (start us, length us, event | category | flops | bytes accessed | tf_op | source)
XLA Modules:
  0.0 526.0 jit_solution(14262006590394135632)
XLA Ops:
  7.2 1.2 compare_select_fusion.2
  8.5 0.8 pad_maximum_fusion.1
  9.4 1.3 fusion.30
  12.0 1.5 constant_dynamic-slice_fusion.3
  16.0 1.5 fusion.43
  19.4 65.3 %all-gather.5.cloned.1.call-done = bf16[64,1,200,3,128]{4,2,3,1,0:T(8,128)(2,1)} async-done(((bf16[2,1,200,3,128]{4,2,3,1,0:T(8,128)(2,1)}), bf16[64,1,200,3,128]{4,2,3,1,0:T(8,128)(2,1)}) %all-gather.5.cloned.1.call-update) | async-done | bytes 9830416 | tf_op jit(solution)/shard_map/all_gather | solution.py:74
  84.7 9.3 %fusion.39 = (bf16[32,1,1,200,3,128]{5,3,4,2,1,0:T(8,128)(2,1)}, bf16[32,1,1,200,3,128]{5,3,4,2,1,0:T(8,128)(2,1)}) fusion(bf16[32,2,1,200,3,128]{5,3,4,2,1,0:T(8,128)(2,1)} %bitcast.230), kind=kLoop, calls=%fused_computation.131 | loop fusion | bytes 19660800 | tf_op jit(solution)/shard_map/slice | solution.py:75
  94.1 1.0 select_bitcast_fusion.3
  95.1 0.9 rev.4
  96.1 1.0 bitcast_select_fusion
  97.2 0.3 slice_bitcast_fusion.1
  97.5 0.3 maximum_bitcast_fusion
  97.8 1.3 copy.28
  99.2 0.2 all-reduce.3.cloned.1.call-start
  100.7 0.9 squeeze.55
  101.6 1.1 reshape.540
  102.7 0.6 broadcast_multiply_fusion.5
  103.3 0.6 fusion.42
  103.9 0.7 fusion.40
  104.6 0.7 fusion.41
  105.3 52.3 %all-gather.7.cloned.1.call-done = bf16[64,1,200,3,14]{2,4,3,1,0:T(8,128)(2,1)} async-done(((bf16[2,1,200,3,14]{2,4,3,1,0:T(8,128)(2,1)}), bf16[64,1,200,3,14]{2,4,3,1,0:T(8,128)(2,1)}) %all-gather.7.cloned.1.call-update) | async-done | bytes 1075216 | tf_op jit(solution)/shard_map/all_gather | solution.py:85
  157.6 28.8 %copy.29 = bf16[64,1,200,3,14]{3,2,4,0,1:T(8,128)(2,1)} copy(bf16[64,1,200,3,14]{2,4,3,1,0:T(8,128)(2,1)} %all-gather.7.cloned.1.call-done) | data formatting | bytes 2150400 | tf_op jit(solution)/shard_map/all_gather | solution.py:85
  186.4 30.0 %fusion.38 = (bf16[32,1,1,200,3,14]{4,3,5,2,1,0:T(8,128)(2,1)}, bf16[32,1,1,200,3,14]{4,3,5,2,1,0:T(8,128)(2,1)}) fusion(bf16[32,2,1,200,3,14]{4,3,5,2,1,0:T(8,128)(2,1)} %bitcast.229), kind=kLoop, calls=%fused_computation.130 | loop fusion | bytes 2150400 | tf_op jit(solution)/shard_map/slice | solution.py:86
  216.3 1.4 select_bitcast_fusion
  218.1 1.8 maximum_convert_fusion
  220.3 11.7 %fusion.37 = (f32[8,128]{1,0:T(8,128)S(1)}, f32[1,200,8,128]{3,1,2,0:T(8,128)S(1)}) fusion(f32[1,200,14,134]{3,1,2,0:T(8,128)S(1)} %maximum_convert_fusion, f32[200]{0:T(256)S(1)} %bitcast.247, f32[200]{0:T(256)S(1)} %bitcast.248, f32[200]{0:T(256)S(1)} %bitcast.250, f32[200]{0:T(256)S(1)} %bitcast.251, f32[200]{0:T(256)S(1)} %bitcast.252, ...), kind=kLoop, calls=%fused_computation.129 | loop fusion | flops 20069376 | bytes 41003296 | tf_op jit(solution)/shard_map/reduce_sum | solution.py:99
  232.4 0.6 fusion.22
  233.1 0.3 copy-done.53
  233.4 1.5 fusion.28
  234.9 0.9 copy-done.6
  235.8 0.3 fusion.20
  236.1 1.7 fusion.5
  237.8 1.8 fusion.26
  239.6 1.5 fusion.17
  241.1 1.6 fusion.13
  242.7 1.6 multiply_reduce_fusion.49
  244.3 6.1 %multiply_reduce_fusion = (f32[200]{0:T(256)S(1)}, f32[200]{0:T(256)S(1)}, f32[200]{0:T(256)S(1)}, f32[200]{0:T(256)S(1)}, f32[200]{0:T(256)S(1)}, /*index=5*/f3...) fusion(f32[1,200,14,134]{3,1,2,0:T(8,128)S(1)} %maximum_convert, ...), kind=kLoop, calls=%fused_computation.30 | loop fusion | flops 8802800 | bytes 17234784 | tf_op jit(solution)/shard_map/reduce_sum | solution.py:137
  250.4 0.9 copy-done.2
  251.3 4.7 multiply_reduce_fusion.18
  256.1 4.6 multiply_reduce_fusion.36
  260.7 0.2 copy.34
  260.8 0.2 stack.223
  261.0 76.9 %psum.23 = f32[200,49]{0,1:T(8,128)S(1)} all-reduce(f32[200,49]{0,1:T(8,128)S(1)} %stack.223), channel_id=1, replica_groups=mesh['ens'=8,'tile'=32] {'ens','tile'}, use_global_device_ids=true, to_apply=%region_56.57 | all-reduce | flops 9800 | bytes 78400 | tf_op jit(solution)/shard_map/psum | solution.py:144
  337.9 0.6 broadcast_multiply_fusion.2
  338.5 2.4 add_convert_fusion
  340.9 174.4 %all-reduce.3.cloned.1.call-done = (f32[200,800]{1,0:T(8,128)}, f32[800,200]{0,1:T(8,128)}) async-done(((f32[200,800]{1,0:T(8,128)}, f32[800,200]{0,1:T(8,128)}), (f32[200,800]{1,0:T(8,128)}, f32[800,200]{0,1:T(8,128)})) %all-reduce.3.cloned.1.call-update) | async-done | bytes 1280016 | tf_op jit(solution)/shard_map/psum | solution.py:144
  515.4 2.0 broadcast_multiply_fusion
  517.4 2.0 broadcast_multiply_fusion.1
  (120 shorter events, 0.8 us)
Async XLA Ops:
  7.2 225.3 %copy-start = (bf16[200,800]{1,0:T(8,128)(2,1)S(1)}, bf16[200,800]{1,0:T(8,128)(2,1)}, u32[]{:S(2)}) copy-start(bf16[200,800]{1,0:T(8,128)(2,1)} %param.17) | copy-start | bytes 960004
  7.2 77.5 %all-gather.5.cloned.1.call-start = ((), (), s32[]{:S(2)}) async-start(), calls=%async_computation | async-start | bytes 10137600 | tf_op jit(solution)/shard_map/all_gather | solution.py:74
  8.5 88.6 %copy-start.3 = (bf16[1,200,8,128]{3,1,2,0:T(8,128)(2,1)}, bf16[1,200,8,128]{3,1,2,0:T(8,128)(2,1)S(1)}, u32[]{:S(2)}) copy-start(bf16[1,200,8,128]{3,1,2,0:T(8,128)(2,1)S(1)} %compare_select_fusion.2) | copy-start | bytes 1228804
  9.3 148.2 %all-gather.7.cloned.1.call-start = ((), (), s32[]{:S(2)}) async-start(), calls=%async_computation.1 | async-start | bytes 1622016 | tf_op jit(solution)/shard_map/all_gather | solution.py:85
  97.1 3.5 copy-start.4
  97.4 4.2 copy-start.9
  97.4 5.3 %copy-start.12 = (f32[200]{0:T(256)S(1)}, f32[200]{0:T(256)}, u32[]{:S(2)}) copy-start(f32[200]{0:T(256)} %param.19) | copy-start | bytes 2404
  97.5 5.8 %copy-start.10 = (f32[200,49]{0,1:T(8,128)S(1)}, f32[200,49]{0,1:T(8,128)}, u32[]{:S(2)}) copy-start(f32[200,49]{0,1:T(8,128)} %param.15) | copy-start | bytes 117604
  99.2 416.2 %all-reduce.3.cloned.1.call-start = ((), (), s32[]{:S(2)}) async-start(), calls=%async_computation.2 | async-start | bytes 2867200 | tf_op jit(solution)/shard_map/psum | solution.py:144
  217.8 2.2 copy-start.14
  217.8 2.2 copy-start.15
  217.8 2.2 copy-start.16
  217.8 2.2 copy-start.17
  217.8 2.2 copy-start.18
  217.8 2.2 copy-start.19
  217.8 2.2 copy-start.20
  217.8 2.2 copy-start.21
  217.8 2.2 copy-start.22
  217.9 2.2 copy-start.23
  217.9 2.2 copy-start.24
  217.9 2.2 copy-start.25
  217.9 2.2 copy-start.26
  217.9 2.2 copy-start.27
  217.9 2.2 copy-start.28
  217.9 2.2 copy-start.29
  217.9 2.2 copy-start.30
  217.9 2.2 copy-start.31
  217.9 2.2 copy-start.32
  218.0 2.2 copy-start.33
  218.0 2.2 copy-start.34
  218.0 2.2 copy-start.35
  218.0 2.2 copy-start.36
  218.0 2.2 copy-start.37
  218.0 2.2 copy-start.38
  218.0 2.2 copy-start.39
  218.0 2.2 copy-start.40
  218.0 2.2 copy-start.41
  218.0 2.2 copy-start.42
  218.1 2.2 copy-start.43
  218.1 2.2 copy-start.44
  218.1 2.2 copy-start.45
  218.1 2.2 copy-start.46
  220.3 11.9 %copy-start.13 = (f32[200]{0:T(256)S(1)}, f32[200]{0:T(256)}, u32[]{:S(2)}) copy-start(f32[200]{0:T(256)} %param.16) | copy-start | bytes 2404
  233.3 2.4 copy-start.5
  233.4 2.4 copy-start.8
  233.4 2.4 copy-start.11
  233.4 2.4 copy-start.52
  256.1 4.6 copy-start.7
  (9 other events, 15.0 us)
Sparse Core Ops, SparseCore 0:
  10.4 74.2 all-gather.4
  99.3 58.2 all-gather.6
  256.2 259.1 all-reduce.2
where the time goes:
time: 528 us; the launch traced here: 526 us
  waiting for transfers between devices  292 us (55%)
  local copies, waits for them, and re-layouts  80.3 us (15%)
  blocking collectives  76.9 us (15%)
  other arithmetic  45.9 us (9%)
  between operations  21.6 us (4%)
  matrix products  8.73 us (2%)
    psum x1, waiting for transfers between devices, local(): lax.psum((part_in, part_out, part_kernel), ('ens', 'tile'))  174 us
    psum x1, blocking collectives, local(): lax.psum((part_in, part_out, part_kernel), ('ens', 'tile'))  76.9 us
    all_gather x1, waiting for transfers between devices, local(): pieces = lax.all_gather(row_strips, 'tile', axis=0, tiled=True)  65.3 us
    all_gather x1, waiting for transfers between devices, local(): pieces = lax.all_gather(side_cols, 'tile', axis=0, tiled=True)  52.3 us
    slice x1, local copies, waits for them, and re-layouts, local(): west_part = take_slot(held[0], pieces[:, 1], west_slot)  30 us
    all_gather x1, local copies, waits for them, and re-layouts, local(): pieces = lax.all_gather(side_cols, 'tile', axis=0, tiled=True)  28.8 us
    reduce_sum x3, other arithmetic, local(): jnp.sum(grad_conv * extended[:, :, row_off:row_off + row_count, col_off:c...  15.4 us
    reduce_sum x1, other arithmetic, local(): chan_mean = jnp.mean(conv_out, axis=1, keepdims=True)  11.7 us
  transfers between devices with their start and end apart: 3, of which 3 were waited for; matrix products, arithmetic and copies ran while one was open for 3% of the time, Pallas kernels for 0%

commit v1 on v0

--- a/solution.py
+++ b/solution.py
@@ -1,3 +1,4 @@
+import functools
 import jax
 import jax.numpy as jnp
 from jax import lax
@@ -7,6 +8,16 @@
 root_half = 0.7071067811865476
 gauss_norm = 0.3989422804014327
 norm_epsilon = 1e-06
+
+
+def meet_copies(sheet, in_dim):
+    e_now = jnp.stack([sheet for _ in range(lax.axis_size("tile"))], axis=0)
+    out_arr = lax.all_to_all(e_now, "tile", 0, 0)
+    value_now = jnp.concatenate(out_arr, axis=in_dim)
+    return value_now
+
+
+name_roots_over_axis = functools.partial(meet_copies, in_dim=0)
 
 
 def gelu_value(values):
@@ -71,7 +82,7 @@
     zero_rows = jnp.zeros((members, channels, 3, col_count), jnp.bfloat16)
     row_strips = jnp.stack([masked[:, :, :3, :], masked[:, :, row_count - 3 :, :]], axis=0)[None]
     held = (zero_rows, zero_rows, zero_rows)
-    pieces = lax.all_gather(row_strips, "tile", axis=0, tiled=True)
+    pieces = name_roots_over_axis(row_strips)
     lower_rows = take_slot(held[0], pieces[:, 0], north_slot)
     upper_rows = take_slot(held[1], pieces[:, 1], north_slot)
     below_rows = take_slot(held[2], pieces[:, 1], south_slot)

time: 528 us -> 658 us (1.25)
  waiting for transfers between devices: 292 us -> 443 us
  local copies, waits for them, and re-layouts: 80.3 us -> 61.6 us
  other arithmetic: 45.9 us -> 35.1 us
  starting transfers between devices: 0.3 us -> 9.08 us
    all_to_all x0 -> x1, waiting for transfers between devices: none -> 210 us  [meet_copies(): out_arr = lax.all_to_all(e_now, 'tile', 0, 0)]
    all_gather x1 -> x0, waiting for transfers between devices: 65.3 us -> none  [local(): pieces = lax.all_gather(row_strips, 'tile', axis=0, tiled=True)]
    all_gather x1 -> x0, local copies, waits for them, and re-layouts: 28.8 us -> none  [local(): pieces = lax.all_gather(side_cols, 'tile', axis=0, tiled=True)]
    slice x1, local copies, waits for them, and re-layouts: 30 us -> 1.48 us  [local(): west_part = take_slot(held[0], pieces[:, 1], west_slot)]
    all_to_all x0 -> x1, local copies, waits for them, and re-layouts: none -> 24.6 us  [meet_copies(): out_arr = lax.all_to_all(e_now, 'tile', 0, 0)]
    all_to_all x0 -> x1, starting transfers between devices: none -> 9 us  [meet_copies(): out_arr = lax.all_to_all(e_now, 'tile', 0, 0)]
  transfers between devices with their start and end apart: 3 -> 3, of which waited for: 3 -> 3; matrix products, arithmetic and copies ran while one was open for 3% -> 2% of each run, Pallas kernels for 0% -> 0%
where the time goes in v1:
time: 658 us; the launch traced here: 656 us
  waiting for transfers between devices  443 us (67%)
  blocking collectives  76.6 us (12%)
  local copies, waits for them, and re-layouts  61.6 us (9%)
  other arithmetic  35.1 us (5%)
  between operations  22.1 us (3%)
  matrix products  9.25 us (1%)
  starting transfers between devices  9.08 us (1%)
    all_to_all x1, waiting for transfers between devices, meet_copies(): out_arr = lax.all_to_all(e_now, 'tile', 0, 0)  210 us
    psum x1, waiting for transfers between devices, local(): lax.psum((part_in, part_out, part_kernel), ('ens', 'tile'))  177 us
    psum x1, blocking collectives, local(): lax.psum((part_in, part_out, part_kernel), ('ens', 'tile'))  76.6 us
    all_gather x1, waiting for transfers between devices, local(): pieces = lax.all_gather(side_cols, 'tile', axis=0, tiled=True)  55.1 us
    all_to_all x1, local copies, waits for them, and re-layouts, meet_copies(): out_arr = lax.all_to_all(e_now, 'tile', 0, 0)  24.6 us
  transfers between devices with their start and end apart: 3, of which 3 were waited for; matrix products, arithmetic and copies ran while one was open for 2% of the time, Pallas kernels for 0%

profile of v1, /device:TPU:8, one launch (start us, length us, event | category | flops | bytes accessed | tf_op | source)
XLA Modules:
  0.0 656.1 jit_solution(14268149734547880217)
XLA Ops:
  7.2 1.6 copy.45
  8.8 0.8 copy.44
  10.0 0.4 maximum_bitcast_fusion
  10.7 5.1 stack.177
  15.8 9.0 %all-to-all-start = ((bf16[32,1,2,1,200,3,128]{6,4,5,3,2,1,0:T(8,128)(2,1)}), bf16[32,1,2,1,200,3,128]{6,4,5,3,2,1,0:T(8,128)(2,1)}, u32[]{:S(2)}, u32[]{:S(2)}) async-start(bf16[32,1,2,1,200,3,128]{6,4,5,3,2,1,0:T(8,128)(2,1)} %stack.177), calls=%async_computation | async-start | bytes 19660800 | tf_op jit(solution)/shard_map/all_to_all | solution.py:15
  24.9 0.6 fusion.31
  26.8 0.6 constant_dynamic-slice_fusion.3
  30.0 0.7 fusion.44
  32.6 210.3 %all-to-all-done = bf16[32,1,2,1,200,3,128]{6,4,5,3,2,1,0:T(8,128)(2,1)} async-done(((bf16[32,1,2,1,200,3,128]{6,4,5,3,2,1,0:T(8,128)(2,1)}), bf16[32,1,2,1,200,3,128]{6,4,5,3,2,1,0:T(8,128)(2,1)}, u32[]{:S(2)}, u32[]{:S(2)}) %all-to-all-start) | async-done | bytes 9830432 | tf_op jit(solution)/shard_map/all_to_all | solution.py:15
  242.9 24.6 %copy.47 = bf16[32,1,2,1,200,3,128]{4,5,6,2,0,3,1:T(4,128)(2,1)} copy(bf16[32,1,2,1,200,3,128]{6,4,5,3,2,1,0:T(8,128)(2,1)} %all-to-all-done) | data formatting | bytes 19660800 | tf_op jit(solution)/shard_map/all_to_all | solution.py:15
  267.5 13.1 %fusion.39 = (bf16[32,1,1,200,3,128]{3,4,5,2,1,0:T(4,128)(2,1)}, bf16[32,1,1,200,3,128]{3,4,5,2,1,0:T(4,128)(2,1)S(1)}) fusion(bf16[32,2,1,200,3,128]{3,4,5,2,1,0:T(4,128)(2,1)} %bitcast.223), kind=kLoop, calls=%fused_computation.130 | loop fusion | bytes 19660800 | tf_op jit(solution)/shard_map/slice | solution.py:86
  280.8 0.6 rev.4
  281.4 1.1 bitcast_select_fusion
  282.6 0.7 copy-done.7
  283.3 0.6 maximum_bitcast_fusion.1
  285.3 0.9 squeeze.55
  286.2 1.1 reshape.547
  287.3 0.6 broadcast_multiply_fusion.5
  287.9 0.7 fusion.41
  288.5 0.7 fusion.42
  289.2 55.1 %all-gather.3.cloned.1.call-done = bf16[64,1,200,3,14]{2,4,3,1,0:T(8,128)(2,1)} async-done(((bf16[2,1,200,3,14]{2,4,3,1,0:T(8,128)(2,1)}), bf16[64,1,200,3,14]{2,4,3,1,0:T(8,128)(2,1)}) %all-gather.3.cloned.1.call-update) | async-done | bytes 1075216 | tf_op jit(solution)/shard_map/all_gather | solution.py:96
  344.5 1.5 fusion.40
  346.1 1.5 maximum_convert_fusion
  347.9 8.8 %fusion.38 = (f32[8,128]{0,1:T(8,128)S(1)}, f32[1,200,8,128]{1,2,3,0:T(8,128)S(1)}) fusion(f32[1,200,14,134]{1,2,3,0:T(8,128)S(1)} %maximum_convert_fusion, f32[200]{0:T(256)S(1)} %bitcast.243, f32[200]{0:T(256)S(1)} %bitcast.244, f32[200]{0:T(256)S(1)} %bitcast.246, f32[200]{0:T(256)S(1)} %bitcast.247, f32[200]{0:T(256)S(1)} %bitcast.248, ...), kind=kLoop, calls=%fused_computation.129 | loop fusion | flops 20069376 | bytes 41003296 | tf_op jit(solution)/shard_map/reduce_sum | solution.py:110
  356.8 0.4 multiply_reduce_fusion.50
  357.2 0.5 copy-done.1
  357.7 1.2 multiply_convert_fusion
  358.9 1.6 copy.48
  360.5 0.6 fusion.22
  361.5 1.5 fusion.28
  363.0 0.9 copy-done.5
  364.3 1.7 fusion.5
  366.0 1.8 fusion.26
  367.8 1.6 fusion.13
  369.4 2.0 fusion.17
  371.4 1.0 copy.53
  372.5 2.6 copy.49
  375.0 2.0 multiply_reduce_fusion.49
  377.2 4.6 multiply_reduce_fusion
  381.8 1.0 copy-done.2
  382.8 3.1 multiply_reduce_fusion.18
  385.9 3.1 multiply_reduce_fusion.36
  389.4 76.6 %psum.23 = f32[200,49]{0,1:T(8,128)S(1)} all-reduce(f32[200,49]{0,1:T(8,128)S(1)} %stack.230), channel_id=1, replica_groups=mesh['ens'=8,'tile'=32] {'ens','tile'}, use_global_device_ids=true, to_apply=%region_56.57 | all-reduce | flops 9800 | bytes 78400 | tf_op jit(solution)/shard_map/psum | solution.py:155
  466.0 0.6 broadcast_multiply_fusion.4
  466.6 1.5 add_convert_fusion
  468.1 177.1 %all-reduce.3.cloned.1.call-done = (f32[200,800]{1,0:T(8,128)}, f32[800,200]{0,1:T(8,128)}) async-done(((f32[200,800]{1,0:T(8,128)}, f32[800,200]{0,1:T(8,128)}), (f32[200,800]{1,0:T(8,128)}, f32[800,200]{0,1:T(8,128)})) %all-reduce.3.cloned.1.call-update) | async-done | bytes 1280016 | tf_op jit(solution)/shard_map/psum | solution.py:155
  645.2 2.0 broadcast_multiply_fusion.1
  647.2 2.0 broadcast_multiply_fusion
  (130 shorter events, 2.5 us)
Async XLA Ops:
  7.2 353.3 %copy-start = (bf16[200,800]{1,0:T(8,128)(2,1)S(1)}, bf16[200,800]{1,0:T(8,128)(2,1)}, u32[]{:S(2)}) copy-start(bf16[200,800]{1,0:T(8,128)(2,1)} %param.17) | copy-start | bytes 960004
  15.8 9.1 %copy-start.20 = (s32[32]{0:T(128)S(1)}, s32[32]{0:T(128)}, u32[]{:S(2)}) copy-start(s32[32]{0:T(128)} %param.14) | copy-start | bytes 388
  15.8 11.0 %copy-start.55 = (s32[32,5]{0,1:T(8,128)S(1)}, s32[32,5]{0,1:T(8,128)}, u32[]{:S(2)}) copy-start(s32[32,5]{0,1:T(8,128)} %param.13) | copy-start | bytes 1924
  15.8 227.1 %all-to-all-start = ((bf16[32,1,2,1,200,3,128]{6,4,5,3,2,1,0:T(8,128)(2,1)}), bf16[32,1,2,1,200,3,128]{6,4,5,3,2,1,0:T(8,128)(2,1)}, u32[]{:S(2)}, u32[]{:S(2)}) async-start(bf16[32,1,2,1,200,3,128]{6,4,5,3,2,1,0:T(8,128)(2,1)} %stack.177), calls=%async_computation | async-start | bytes 19660800 | tf_op jit(solution)/shard_map/all_to_all | solution.py:15
  24.8 319.4 %all-gather.3.cloned.1.call-start = ((), (), s32[]{:S(2)}) async-start(), calls=%async_computation.1 | async-start | bytes 1622016 | tf_op jit(solution)/shard_map/all_gather | solution.py:96
  280.6 4.7 copy-start.3
  280.6 5.6 copy-start.12
  280.6 6.7 %copy-start.18 = (f32[200]{0:T(256)S(1)}, f32[200]{0:T(256)}, u32[]{:S(2)}) copy-start(f32[200]{0:T(256)} %param.19) | copy-start | bytes 2404
  280.6 7.3 %copy-start.13 = (f32[200,49]{0,1:T(8,128)S(1)}, f32[200,49]{0,1:T(8,128)}, u32[]{:S(2)}) copy-start(f32[200,49]{0,1:T(8,128)} %param.15) | copy-start | bytes 117604
  280.8 65.2 %copy-start.9 = (bf16[1,200,3,128]{1,2,3,0:T(4,128)(2,1)}, bf16[1,200,3,128]{1,2,3,0:T(4,128)(2,1)S(1)}, u32[]{:S(2)}) copy-start(bf16[1,200,3,128]{1,2,3,0:T(4,128)(2,1)S(1)} %get-tuple-element.60) | copy-start | bytes 460804
  283.9 361.3 %all-reduce.3.cloned.1.call-start = ((), (), s32[]{:S(2)}) async-start(), calls=%async_computation.2 | async-start | bytes 2867200 | tf_op jit(solution)/shard_map/psum | solution.py:155
  344.2 3.4 copy-start.21
  344.2 3.4 copy-start.22
  344.2 3.4 copy-start.23
  344.2 3.4 copy-start.24
  344.3 3.4 copy-start.25
  344.3 3.4 copy-start.26
  344.3 3.4 copy-start.27
  344.3 3.4 copy-start.28
  344.3 3.4 copy-start.29
  344.3 3.4 copy-start.30
  344.3 3.4 copy-start.31
  344.3 3.4 copy-start.32
  344.3 3.4 copy-start.33
  344.3 3.4 copy-start.34
  344.4 3.4 copy-start.35
  344.4 3.4 copy-start.36
  344.4 3.4 copy-start.37
  344.4 3.4 copy-start.38
  344.4 3.4 copy-start.39
  344.4 3.4 copy-start.40
  344.4 3.4 copy-start.41
  344.4 3.4 copy-start.42
  344.4 3.4 copy-start.43
  344.4 3.4 copy-start.44
  344.5 3.4 copy-start.45
  344.5 3.4 copy-start.46
  344.5 3.4 copy-start.47
  344.5 3.4 copy-start.48
  344.5 3.4 copy-start.49
  344.5 3.4 copy-start.50
  344.5 3.4 copy-start.51
  344.5 3.4 copy-start.52
  344.5 3.4 copy-start.53
  347.9 9.8 %copy-start.15 = (f32[200]{0:T(256)S(1)}, f32[200]{0:T(256)}, u32[]{:S(2)}) copy-start(f32[200]{0:T(256)} %param.16) | copy-start | bytes 2404
  361.5 2.5 copy-start.17
  361.5 2.5 copy-start.19
  385.9 3.1 copy-start.6
  (12 other events, 20.4 us)
Sparse Core Ops, SparseCore 0:
  284.1 60.1 all-gather.2
  386.1 259.1 all-reduce.2
